TPU v7x, 128 devices: a whole 4x4x4 slice. The times are simulated.
128 devices in a mesh: feed: 32 (over y_hi, x, z), tm: 4 (over y_lo, core).
Axes of the slice: x: 4, y: 4 (y_hi: 2, y_lo: 2; y = y_hi * 2 + y_lo), z: 4, core: 2. Of those that a mesh axis runs over, the one named last changes fastest.
Arguments:
- voltages: int32 [512, 524288], P('feed', 'tm'), may hold values from -128 to 127, as said below
- pfb_taps: float32 [16, 2048], replicated, may hold values from -3 to 3
- feed_flags: int32 [512], P('feed'), may hold values 0 or 1
Outputs:
- visibility: float32 [1024, 2, 512, 512], P(('feed', 'tm'))
Inputs may be any that keep to these rules, and one draw needn't show every extreme that they name: `voltages`: signed 8-bit sample values.
All inputs are finite; a program needn't handle non-finite values. No bound on the sum of `feed_flags` on one device may be relied on, other than what follows from the above.
Results may differ from a plain program's by a relative error of at most 0.0019.
Values may be sent and summed in bfloat16 or wider, within the bound.
A program may use at most 128 MiB of HBM per device.

v0:
```python
import math

import jax
import jax.numpy as jnp
from jax import lax
from jax.sharding import PartitionSpec as P


def shifted(block, axis, distance):
    devices = range(lax.axis_size(axis))
    route = [(i - distance, i) for i in devices if i - distance in devices]
    return lax.ppermute(block, axis, route)


def dft_tables(frame_len, channels):
    row_index = lax.broadcasted_iota(jnp.int32, (channels, frame_len), 0)
    sample_index = lax.broadcasted_iota(jnp.int32, (channels, frame_len), 1)
    phase_step = row_index * sample_index % frame_len
    phase_angle = phase_step.astype(jnp.float32) * (2.0 * math.pi / frame_len)
    dft_table = jnp.concatenate([jnp.cos(phase_angle), -jnp.sin(phase_angle)], axis=0)
    table_high = dft_table.astype(jnp.bfloat16)
    table_low = (dft_table - table_high.astype(jnp.float32)).astype(jnp.bfloat16)
    return (table_high, table_low)


def batched_gram(left_part, right_part):
    numbers = (((2,), (2,)), ((0,), (0,)))
    return lax.dot_general(left_part, right_part, numbers, preferred_element_type=jnp.float32)


def cross_pair(real_rows, imag_rows, real_cols, imag_cols):
    vis_real = batched_gram(real_rows, real_cols) + batched_gram(imag_rows, imag_cols)
    vis_imag = batched_gram(imag_rows, real_cols) - batched_gram(real_rows, imag_cols)
    return (vis_real, vis_imag)


def per_device(voltages, pfb_taps, feed_flags):
    inputs_dev = voltages.shape[0]
    taps_count = pfb_taps.shape[0]
    frame_len = pfb_taps.shape[1]
    spec_dev = voltages.shape[1] // frame_len
    channels = frame_len // 2
    feed_count = lax.axis_size("feed")
    time_count = lax.axis_size("tm")
    chan_dev = channels // (feed_count * time_count)
    all_inputs = feed_count * inputs_dev
    spectra_total = spec_dev * time_count
    samples = voltages.astype(jnp.bfloat16).reshape(inputs_dev, spec_dev, frame_len)
    rim_frames = samples[:, spec_dev - taps_count + 1 :, :]
    before = shifted(rim_frames, "tm", 1)
    frames = jnp.concatenate([before, samples], axis=1).astype(jnp.float32) / 128.0
    running = jnp.zeros((inputs_dev, spec_dev, frame_len), jnp.float32)
    for tap_lag in range(taps_count):
        offset = taps_count - 1 - tap_lag
        running = running + pfb_taps[tap_lag] * frames[:, offset : offset + spec_dev, :]
    kept_mask = feed_flags.astype(jnp.float32)[:, None, None]
    filtered = (running * kept_mask).astype(jnp.bfloat16).reshape(inputs_dev * spec_dev, frame_len)
    table_high, table_low = dft_tables(frame_len, channels)
    contract = (((1,), (1,)), ((), ()))
    transformed = lax.dot_general(
        table_high, filtered, contract, preferred_element_type=jnp.float32
    )
    transformed = transformed + lax.dot_general(
        table_low, filtered, contract, preferred_element_type=jnp.float32
    )
    spectra = (
        (transformed / math.sqrt(frame_len))
        .astype(jnp.bfloat16)
        .reshape(2, channels, inputs_dev, spec_dev)
    )
    turned = lax.all_to_all(spectra, ("feed", "tm"), split_axis=1, concat_axis=2, tiled=True)
    turned = turned.reshape(2, chan_dev, feed_count, time_count, inputs_dev, spec_dev)
    turned = jnp.transpose(turned, (0, 1, 2, 4, 3, 5)).reshape(
        2, chan_dev, all_inputs, spectra_total
    )
    real_all = turned[0]
    imag_all = turned[1]
    vis_real, vis_imag = cross_pair(real_all, imag_all, real_all, imag_all)
    return jnp.stack([vis_real, vis_imag], axis=1) / spectra_total


def solution(mesh):
    return jax.shard_map(
        per_device,
        mesh=mesh,
        in_specs=(P("feed", "tm"), P(), P("feed")),
        out_specs=P(("feed", "tm"), None, None, None),
        check_vma=False,
    )
```

profile of v0, /device:TPU:7, one launch (start us, length us, event | category | flops | bytes accessed | tf_op | source)
XLA Modules:
  0.0 282.8 jit_solution(15767832720702721144)
XLA Ops:
  0.0 3.8 %convert_element_type.31 = bf16[16,131072]{1,0:T(8,128)(2,1)S(1)} convert(s32[16,131072]{1,0:T(8,128)} %param.3) | non-fusion elementwise | flops 2097152 | bytes 12582912 | tf_op jit(solution)/shard_map/convert_element_type | solution.py:48
  3.8 0.0 copy-start.3
  3.8 0.0 copy-start.4
  3.8 2.3 copy.44
  6.1 0.3 slice.142
  6.5 0.6 copy.32
  7.0 3.8 %collective-permute-start = (bf16[16,15,2048]{2,0,1:T(8,128)(2,1)S(1)}, bf16[16,15,2048]{2,0,1:T(8,128)(2,1)S(1)}, u32[]{:S(2)}, u32[]{:S(2)}) collective-permute-start(bf16[16,15,2048]{2,0,1:T(8,128)(2,1)S(1)} %copy.32), channel_id=1, source_target_pairs={{0,1},{1,2},{2,3},{4,5},{5,6},{6,7},{8,9},{9,10},{10,11},{12,13},{... | collective-permute-start | bytes 2949128 | tf_op jit(solution)/shard_map/ppermute | solution.py:12
  10.8 0.0 copy-done.3
  10.8 0.1 fusion.33
  10.9 0.0 copy-done.4
  10.9 34.9 %sine_negate_fusion = (f32[1024,2048]{1,0:T(8,128)}, f32[1024,2048]{1,0:T(8,128)}) fusion(), kind=kLoop, calls=%fused_computation.48 | loop fusion | flops 31457280 | bytes 16777216 | tf_op jit(solution)/shard_map/neg | solution.py:20
  45.9 0.0 collective-permute-done
  45.9 0.5 copy.33
  46.4 1.8 convert_multiply_fusion
  48.2 16.8 %fusion.8 = bf16[16,64,2048]{2,1,0:T(8,128)(2,1)S(1)} fusion(f32[16,79,2048]{2,1,0:T(8,128)S(1)} %convert_multiply_fusion, f32[16]{0:T(128)S(1)} %convert_element_type.33, f32[2048]{0:T(1024)S(1)} %bitcast.65, f32[2048]{0:T(1024)S(1)} %bitcast.66, f32[2048]{0:T(1024)S(1)} %bitcast.52, f32[2048]{0:T(1024)S(1)} %bitcast.53, f32[2048]{0:T(1024)S(1)} %bitcast.54, ...), kind=kLoop, calls=%fused_computation.15 | loop fusion | flops 69206016 | bytes 138543168 | tf_op jit(solution)/shard_map/convert_element_type | solution.py:57
  65.0 0.0 copy-start.2
  65.0 1.9 copy-done.2
  67.0 15.2 %fusion.25 = f32[2048,1024]{1,0:T(8,128)} fusion(bf16[1024,2048]{1,0:T(8,128)(2,1)S(1)} %bitcast.49, f32[1024,2048]{1,0:T(8,128)} %get-tuple-element.23, f32[1024,2048]{1,0:T(8,128)} %get-tuple-element.24), kind=kOutput, calls=%fused_computation.51 | convolution fusion | flops 8610906112 | bytes 29360128 | tf_op jit(solution)/shard_map/dot_general | solution.py:63
  82.1 29.0 %multiply_convert_fusion = bf16[2048,1024]{1,0:T(8,128)(2,1)} fusion(f32[2048,1024]{1,0:T(8,128)} %fusion.25, bf16[1024,2048]{1,0:T(8,128)(2,1)} %bitcast.50, f32[1024,2048]{1,0:T(8,128)} %get-tuple-element.23, f32[1024,2048]{1,0:T(8,128)} %get-tuple-element.24), kind=kOutput, calls=%fused_computation.47 | convolution fusion | flops 8613003264 | bytes 33554432 | tf_op jit(solution)/shard_map/dot_general | solution.py:60
  111.1 11.5 %reshape.39 = bf16[2,1024,16,64]{3,2,1,0:T(8,128)(2,1)} reshape(bf16[2048,1024]{1,0:T(8,128)(2,1)} %multiply_convert_fusion) | data formatting | bytes 8388608 | tf_op jit(solution)/shard_map/reshape | solution.py:69
  122.7 8.1 %copy.46 = bf16[2,1024,16,64]{3,2,0,1:T(8,128)(2,1)} copy(bf16[2,1024,16,64]{3,2,1,0:T(8,128)(2,1)} %reshape.39) | data formatting | bytes 8388608 | tf_op jit(solution)/shard_map/reshape | solution.py:69
  130.7 14.3 %reshape.40 = bf16[128,2,8192]{2,1,0:T(2,128)(2,1)} reshape(bf16[1024,2,16,64]{3,2,1,0:T(8,128)(2,1)} %bitcast.44) | data formatting | bytes 8388608
  145.0 65.1 %all_to_all.15 = bf16[128,2,8192]{2,1,0:T(2,128)(2,1)} all-to-all(bf16[128,2,8192]{2,1,0:T(2,128)(2,1)} %reshape.40), channel_id=1, replica_groups=mesh['feed'=32,'tm'=4] {'feed','tm'}, dimensions={0} | all-to-all | bytes 8388608 | tf_op jit(solution)/shard_map/all_to_all | solution.py:71
  210.2 14.6 %reshape.41 = bf16[1024,2,16,64]{3,2,1,0:T(8,128)(2,1)} reshape(bf16[128,2,8192]{2,1,0:T(2,128)(2,1)} %all_to_all.15) | data formatting | bytes 8388608
  224.7 8.8 %copy.37 = bf16[2,8,128,16,64]{4,3,2,1,0:T(8,128)(2,1)} copy(bf16[2,8,128,16,64]{4,3,0,1,2:T(8,128)(2,1)} %bitcast.45) | data formatting | bytes 8388608 | tf_op jit(solution)/shard_map/all_to_all | solution.py:71
  233.6 5.9 %fusion.32 = (bf16[1,8,32,16,4,64]{5,3,4,2,1,0:T(8,128)(2,1)S(1)}, bf16[1,8,32,16,4,64]{5,3,4,2,1,0:T(8,128)(2,1)}) fusion(bf16[2,8,32,16,4,64]{5,3,4,2,1,0:T(8,128)(2,1)} %bitcast.43), kind=kLoop, calls=%fused_computation.56 | loop fusion | bytes 8388608 | tf_op jit(solution)/shard_map/slice | solution.py:76
  239.4 4.2 %copy.38 = bf16[1,8,32,16,4,64]{5,4,3,2,1,0:T(4,128)(2,1)} copy(bf16[1,8,32,16,4,64]{5,3,4,2,1,0:T(8,128)(2,1)S(1)} %get-tuple-element.5) | data formatting | bytes 4194304 | tf_op jit(solution)/shard_map/slice | solution.py:76
  243.7 6.0 %squeeze.6 = bf16[8,512,256]{2,1,0:T(8,128)(2,1)S(1)} reshape(bf16[1,8,32,16,4,64]{5,4,3,2,1,0:T(4,128)(2,1)} %copy.38) | data formatting | bytes 4194304 | tf_op jit(solution)/shard_map/squeeze | solution.py:76
  249.6 6.6 %copy.39 = bf16[1,8,32,16,4,64]{5,4,3,2,1,0:T(4,128)(2,1)} copy(bf16[1,8,32,16,4,64]{5,3,4,2,1,0:T(8,128)(2,1)} %get-tuple-element.6) | data formatting | bytes 4194304 | tf_op jit(solution)/shard_map/slice | solution.py:77
  256.2 7.0 %squeeze.7 = bf16[8,512,256]{2,1,0:T(8,128)(2,1)} reshape(bf16[1,8,32,16,4,64]{5,4,3,2,1,0:T(4,128)(2,1)} %copy.39) | data formatting | bytes 4194304 | tf_op jit(solution)/shard_map/squeeze | solution.py:77
  263.2 0.0 copy-start
  263.2 1.3 fusion.34
  264.4 0.3 copy-done
  264.8 1.3 fusion.35
  266.0 4.7 %subtract_bitcast_fusion = f32[8,1,512,512]{3,2,0,1:T(8,128)} fusion(f32[8,512,512]{2,1,0:T(8,128)S(1)} %fusion.35, bf16[8,512,256]{2,1,0:T(8,128)(2,1)S(1)} %squeeze.6, bf16[8,512,256]{2,1,0:T(8,128)(2,1)S(1)} %copy-done), kind=kOutput, calls=%fused_computation.45 | convolution fusion | flops 1075838976 | bytes 20971520 | tf_op jit(solution)/shard_map/dot_general | solution.py:28
  270.8 0.0 copy-start.1
  270.8 1.3 add_bitcast_fusion
  272.1 2.1 copy-done.1
  274.2 2.0 maximum_multiply_fusion
  276.2 6.4 %copy.40 = f32[8,2,512,512]{3,2,1,0:T(8,128)} copy(f32[8,2,512,512]{3,2,0,1:T(8,128)S(1)} %maximum_multiply_fusion) | data formatting | bytes 33554432 | tf_op jit(solution)/shard_map/div | solution.py:79
  (1 shorter events, 0.0 us)
Async XLA Ops:
  3.8 7.0 %copy-start.3 = (f32[16,2048]{1,0:T(8,128)S(1)}, f32[16,2048]{1,0:T(8,128)}, u32[]{:S(2)}) copy-start(f32[16,2048]{1,0:T(8,128)} %param.4) | copy-start | bytes 393220
  3.8 7.1 %copy-start.4 = (s32[16]{0:T(128)S(1)}, s32[16]{0:T(128)}, u32[]{:S(2)}) copy-start(s32[16]{0:T(128)} %param.5) | copy-start | bytes 196
  7.0 38.8 %collective-permute-start = (bf16[16,15,2048]{2,0,1:T(8,128)(2,1)S(1)}, bf16[16,15,2048]{2,0,1:T(8,128)(2,1)S(1)}, u32[]{:S(2)}, u32[]{:S(2)}) collective-permute-start(bf16[16,15,2048]{2,0,1:T(8,128)(2,1)S(1)} %copy.32), channel_id=1, source_target_pairs={{0,1},{1,2},{2,3},{4,5},{5,6},{6,7},{8,9},{9,10},{10,11},{12,13},{... | collective-permute-start | bytes 2949128 | tf_op jit(solution)/shard_map/ppermute | solution.py:12
  65.0 1.9 copy-start.2
  263.2 1.6 copy-start
  270.8 3.4 %copy-start.1 = (f32[8,1,512,512]{3,2,0,1:T(8,128)S(1)}, f32[8,1,512,512]{3,2,0,1:T(8,128)}, u32[]{:S(2)}) copy-start(f32[8,1,512,512]{3,2,0,1:T(8,128)} %subtract_bitcast_fusion) | copy-start | bytes 25165828
where the time goes:
time: 288 us; the launch traced here: 283 us
  local copies, waits for them, and re-layouts  101 us (35%)
  blocking collectives  65.1 us (23%)
  other arithmetic  59.4 us (21%)
  matrix products  52.7 us (18%)
  starting transfers between devices  3.77 us (1%)
    all_to_all x1, blocking collectives, per_device(): lax.all_to_all(spectra, ('feed', 'tm'), split_axis=1, concat_axis=2, tile...  65.1 us
    unnamed x13, local copies, waits for them, and re-layouts  35.5 us
    neg x1, other arithmetic, dft_tables(): -jnp.sin(phase_angle)  34.9 us
    dot_general x1, matrix products, per_device(): lax.dot_general(table_high, filtered, contract, preferred_element_type=jn...  29 us
    reshape x2, local copies, waits for them, and re-layouts, per_device(): spectra = (transformed / math.sqrt(frame_len)).astype(jnp.bfloat16).resha...  19.6 us
    convert_element_type x1, other arithmetic, per_device(): (running * kept_mask).astype(jnp.bfloat16)  16.8 us
    dot_general x1, matrix products, per_device(): lax.dot_general(table_low, filtered, contract, preferred_element_type=jnp...  15.2 us
    slice x2, local copies, waits for them, and re-layouts, per_device(): real_all = turned[0]  10.1 us
  transfers between devices with their start and end apart: 1, of which 0 were waited for; matrix products, arithmetic and copies ran while one was open for 12% of the time, Pallas kernels for 0%

commit v1 on v0

v1 whole, which is shorter than its diff:
```python
import functools
import math

import jax
import jax.numpy as jnp
import numpy as np
from jax import lax
from jax.experimental import pallas as pl
from jax.experimental.pallas import tpu as pltpu
from jax.sharding import PartitionSpec as P

MESH = pl.DeviceIdType.MESH
LANES = 128
FRAME = 2048
HALF = FRAME // 2
TAPS = 16
FEEDS, TIMES = 32, 4
DEVICES = FEEDS * TIMES
SPEC = 64
OCT = 8
BLOCKS = SPEC // 16


def link_loads(offset):
    loads = [0] * 6
    for axis, step in enumerate(offset[1:]):
        if step in (1, 2):
            loads[2 * axis] += 1
        if step in (2, 3):
            loads[2 * axis + 1] += 1
    return loads


def send_order():
    left = [
        (c, y, x, z)
        for z in range(4)
        for x in range(4)
        for y in range(4)
        for c in range(2)
        if (c, y, x, z) != (0, 0, 0, 0)
    ]
    mixed = [left[(37 * i + 11) % len(left)] for i in range(len(left))]
    order, total = [], [0] * 6
    while mixed:
        def spread(offset):
            sums = [a + b for a, b in zip(total, link_loads(offset))]
            mean = sum(sums) / 6
            return sum((s - mean) ** 2 for s in sums)

        best = min(mixed, key=spread)
        mixed.remove(best)
        order.append(best)
        total = [a + b for a, b in zip(total, link_loads(best))]
    return order


ORDER = send_order()


def peer(offset, feed, time):
    dc, dy, dx, dz = offset
    y = feed // 16 * 2 + time // 2
    x = lax.rem(feed // 4 % 4 + dx, 4)
    z = lax.rem(feed % 4 + dz, 4)
    y = lax.rem(y + dy, 4)
    c = lax.rem(time % 2 + dc, 2)
    return y // 2 * 16 + x * 4 + z, y % 2 * 2 + c


def phase_tables():
    n = np.arange(HALF)
    coarse = np.exp(-2j * np.pi * ((16 * np.arange(64)[:, None] * n) % FRAME) / FRAME)
    rows = 8 * np.arange(2)[:, None] + 2 * np.arange(4)
    rows = rows.reshape(8)[None, :, None] + np.arange(2)[:, None, None]
    scale = 1.0 / (128 * 16 * math.sqrt(FRAME))
    fine = scale * np.exp(-2j * np.pi * (rows * n % FRAME) / FRAME)
    coarse = np.stack([coarse.real, coarse.imag]).astype(np.float32)
    fine = np.stack([fine.real, fine.imag], axis=1).astype(np.float32)
    return coarse, fine


def channelise(
    volt_hbm, taps_ref, flag_ref, coarse_ref, fine_ref, out_ref,
    volt, edge, halo, table_hi, table_lo, folded, spectra, packed,
    in_sem, halo_send, halo_recv, send_sem, recv_sem, own_sem,
):
    feed, time = lax.axis_index("feed"), lax.axis_index("tm")
    me = feed * TIMES + time

    tail = (SPEC - 16) * FRAME
    loads = []
    for o in range(2):
        loads.append(pltpu.make_async_copy(
            volt_hbm.at[pl.ds(o * OCT, OCT), pl.ds(tail, 16 * FRAME)],
            volt.at[o, :, pl.ds(tail, 16 * FRAME)], in_sem.at[o, 0]))
    for o in range(2):
        loads.append(pltpu.make_async_copy(
            volt_hbm.at[pl.ds(o * OCT, OCT), pl.ds(0, tail)],
            volt.at[o, :, pl.ds(0, tail)], in_sem.at[o, 1]))
    for load in loads:
        load.start()

    barrier = pltpu.get_barrier_semaphore()

    def greet(step, carry):
        other = lax.rem(me + step, DEVICES)
        pl.semaphore_signal(barrier, inc=1, device_id=(other // TIMES, other % TIMES), device_id_type=MESH)
        return carry

    lax.fori_loop(1, DEVICES, greet, 0)

    def make_table(q):
        fine_re, fine_im = fine_ref[q, 0], fine_ref[q, 1]

        def rows(pair, carry):
            parts = []
            for side in range(2):
                a_re = coarse_ref[0, pl.ds(pair * 2 + side, 1), :]
                a_im = coarse_ref[1, pl.ds(pair * 2 + side, 1), :]
                parts.append((a_re * fine_re - a_im * fine_im, a_re * fine_im + a_im * fine_re))
            for c in range(2):
                value = jnp.concatenate([parts[0][c], parts[1][c]], axis=0)
                high = value.astype(jnp.bfloat16)
                low = (value - high.astype(jnp.float32)).astype(jnp.bfloat16)
                at = pl.ds(pl.multiple_of(pair * 16, 16), 16)
                table_hi[q, c, at, :] = high
                table_lo[q, c, at, :] = low
            return carry

        lax.fori_loop(0, 32, rows, 0)

    make_table(0)

    for o in range(2):
        loads[o].wait()

        def pack_edge(nb, carry, o=o):
            for pair in range(8):
                two = []
                for side in range(2):
                    at = pl.multiple_of(tail + (pair * 2 + side) * FRAME + nb * LANES, LANES)
                    two.append(volt[o, :, pl.ds(at, LANES)].astype(jnp.float32))
                lanes = pl.ds(pl.multiple_of(nb * LANES, LANES), LANES)
                edge[o, pair, :, lanes] = jnp.concatenate(two, axis=0).astype(jnp.bfloat16)
            return carry

        lax.fori_loop(0, FRAME // LANES, pack_edge, 0)

    pl.semaphore_wait(barrier, DEVICES - 1)

    def halo_copy(o):
        return pltpu.make_async_remote_copy(
            src_ref=edge.at[o], dst_ref=halo.at[o], send_sem=halo_send.at[o], recv_sem=halo_recv.at[o],
            device_id=(feed, lax.rem(time + 1, TIMES)), device_id_type=MESH)

    @pl.when(time < TIMES - 1)
    def _():
        for o in range(2):
            halo_copy(o).start()

    @pl.when(time == 0)
    def _():
        halo[...] = jnp.zeros_like(halo)

    def filter_block(o, mb, nb, first):
        flag = flag_ref[o]
        sides = []
        for side in range(2):
            lane0 = nb * LANES + side * HALF
            lanes = pl.ds(pl.multiple_of(lane0, LANES), LANES)
            taps = [jnp.broadcast_to(taps_ref[pl.ds(p, 1), lanes], (OCT, LANES)) for p in range(TAPS)]
            sums = [None] * 16
            early = None
            for j in range(-15, 16):
                if first and j < 0:
                    pair, odd = (16 + j) // 2, (16 + j) % 2
                    if odd == 0 or early is None:
                        early = halo[o, pair, :, lanes].astype(jnp.float32)
                    x = early[odd * OCT:(odd + 1) * OCT]
                else:
                    at = pl.multiple_of((mb * 16 + j) * FRAME + lane0, LANES)
                    x = volt[o, :, pl.ds(at, LANES)].astype(jnp.float32)
                for m in range(max(0, j), min(15, j + 15) + 1):
                    term = taps[m - j] * x
                    sums[m] = term if sums[m] is None else sums[m] + term
            value = jnp.stack([s * flag for s in sums])
            value = jnp.swapaxes(value, 0, 1)
            sides.append(value.astype(jnp.bfloat16).astype(jnp.float32))
        rows = pl.ds(pl.multiple_of(mb * 16, 16), 16)
        lanes = pl.ds(pl.multiple_of(nb * LANES, LANES), LANES)
        folded[o, 0, :, rows, lanes] = (sides[0] + sides[1]).astype(jnp.bfloat16)
        folded[o, 1, :, rows, lanes] = (sides[0] - sides[1]).astype(jnp.bfloat16)

    for o in range(2):
        loads[2 + o].wait()

    def later_blocks(step, carry):
        o = step // (8 * (BLOCKS - 1))
        rest = step % (8 * (BLOCKS - 1))
        filter_block(o, 1 + rest // 8, rest % 8, False)
        return carry

    lax.fori_loop(0, 2 * 8 * (BLOCKS - 1), later_blocks, 0)

    lane = lax.broadcasted_iota(jnp.int32, (8, LANES), 1)
    left_half = lane < SPEC

    def exchange(o, q, other_feed, other_time):
        return pltpu.make_async_remote_copy(
            src_ref=packed.at[other_feed * TIMES + other_time, o, q],
            dst_ref=out_ref.at[q, pl.ds(0, 2), time, feed, o],
            send_sem=send_sem, recv_sem=recv_sem, device_id=(other_feed, other_time), device_id_type=MESH)

    def own_copy(o, q):
        return pltpu.make_async_copy(
            packed.at[me, o, q], out_ref.at[q, pl.ds(0, 2), time, feed, o], own_sem)

    def octet(o, carry):
        @pl.when(time > 0)
        def _():
            halo_copy(o).wait_recv()

        def first_block(nb, c):
            filter_block(o, 0, nb, True)
            return c

        lax.fori_loop(0, 8, first_block, 0)

        def parity(q, carry):
            @pl.when((o == 0) & (q == 1))
            def _():
                make_table(1)

            right = folded[o, q].reshape(OCT * SPEC, HALF)
            dims = (((1,), (1,)), ((), ()))
            for c in range(2):
                spectra[c] = lax.dot_general(
                    table_hi[q, c], right, dims, preferred_element_type=jnp.float32
                ) + lax.dot_general(table_lo[q, c], right, dims, preferred_element_type=jnp.float32)

            def turn(g, c):
                rows = pl.ds(pl.multiple_of(g * 8, 8), 8)
                tiles = []
                for pair in range(OCT // 2):
                    re = spectra[0, rows, pair * LANES:(pair + 1) * LANES]
                    im = spectra[1, rows, pair * LANES:(pair + 1) * LANES]
                    tiles.append(jnp.where(left_half, re, pltpu.roll(im, SPEC, 1)))
                    tiles.append(jnp.where(left_half, pltpu.roll(re, SPEC, 1), im))
                tile = jnp.swapaxes(jnp.stack(tiles), 0, 1)
                packed[pl.ds(g * 2, 2), o, q] = tile.reshape(2, 2, 16, LANES).astype(jnp.bfloat16)
                return c

            lax.fori_loop(0, DEVICES // 2, turn, 0)
            for offset in ORDER:
                exchange(o, q, *peer(offset, feed, time)).start()
            own_copy(o, q).start()
            return carry

        lax.fori_loop(0, 2, parity, 0)
        return carry

    lax.fori_loop(0, 2, octet, 0)

    @pl.when(time < TIMES - 1)
    def _():
        for o in range(2):
            halo_copy(o).wait_send()

    everything = pltpu.make_async_remote_copy(
        src_ref=packed.at[pl.ds(0, DEVICES - 1)], dst_ref=packed.at[pl.ds(0, DEVICES - 1)],
        send_sem=send_sem, recv_sem=recv_sem, device_id=(feed, time), device_id_type=MESH)
    everything.wait()
    own = packed.at[0]
    pltpu.make_async_copy(own, own, own_sem).wait()


def gather_spectra(voltages, pfb_taps, flags, coarse, fine):
    vmem = pl.BlockSpec(memory_space=pltpu.VMEM)
    return pl.pallas_call(
        channelise,
        out_shape=jax.ShapeDtypeStruct((2, 2, TIMES, FEEDS, 2, 16, LANES), jnp.bfloat16),
        in_specs=[pl.BlockSpec(memory_space=pl.ANY), vmem, vmem, vmem, vmem],
        out_specs=pl.BlockSpec(memory_space=pl.ANY),
        scratch_shapes=[
            pltpu.VMEM((2, OCT, SPEC * FRAME), jnp.int32),
            pltpu.VMEM((2, 8, 16, FRAME), jnp.bfloat16),
            pltpu.VMEM((2, 8, 16, FRAME), jnp.bfloat16),
            pltpu.VMEM((2, 2, 512, HALF), jnp.bfloat16),
            pltpu.VMEM((2, 2, 512, HALF), jnp.bfloat16),
            pltpu.VMEM((2, 2, OCT, SPEC, HALF), jnp.bfloat16),
            pltpu.VMEM((2, 512, OCT * SPEC), jnp.float32),
            pltpu.VMEM((DEVICES, 2, 2, 2, 16, LANES), jnp.bfloat16),
            pltpu.SemaphoreType.DMA((2, 2)),
            pltpu.SemaphoreType.DMA((2,)),
            pltpu.SemaphoreType.DMA((2,)),
            pltpu.SemaphoreType.DMA,
            pltpu.SemaphoreType.DMA,
            pltpu.SemaphoreType.DMA,
        ],
        compiler_params=pltpu.CompilerParams(
            collective_id=0, has_side_effects=True, vmem_limit_bytes=48 << 20),
        name="channelise",
    )(voltages, pfb_taps, flags, coarse, fine)


def correlate(block_ref, out_ref, left, right):
    which = pl.program_id(2)
    lane = lax.broadcasted_iota(jnp.int32, (8, LANES), 1)

    for other in range(2):
        @pl.when(which == other)
        def _():
            for t in range(TIMES):
                tile = block_ref[0, 0, t].astype(jnp.float32)
                tile = tile[:, :, other * OCT:(other + 1) * OCT, :].reshape(512, LANES)
                cols = slice(t * LANES, (t + 1) * LANES)
                right[:, cols] = tile.astype(jnp.bfloat16)
                sign = jnp.where(lane[:1] < SPEC, 1.0, -1.0)
                left[:, cols] = (pltpu.roll(tile, SPEC, 1) * sign).astype(jnp.bfloat16)

    dims = (((1,), (1,)), ((), ()))
    value = right[...]
    out_ref[0, 0, 0, 0] = lax.dot_general(value, value, dims, preferred_element_type=jnp.float32)
    out_ref[0, 0, 0, 1] = lax.dot_general(left[...], value, dims, preferred_element_type=jnp.float32)


def visibilities(gathered):
    out = pl.pallas_call(
        correlate,
        out_shape=jax.ShapeDtypeStruct((2, 2, 2, 2, 512, 512), jnp.float32),
        grid=(2, 2, 2),
        in_specs=[pl.BlockSpec((1, 1, TIMES, FEEDS, 2, 16, LANES), lambda q, p, j: (q, p, 0, 0, 0, 0, 0))],
        out_specs=pl.BlockSpec((1, 1, 1, 2, 512, 512), lambda q, p, j: (p, j, q, 0, 0, 0)),
        scratch_shapes=[pltpu.VMEM((512, 512), jnp.bfloat16), pltpu.VMEM((512, 512), jnp.bfloat16)],
        compiler_params=pltpu.CompilerParams(vmem_limit_bytes=32 << 20),
        name="correlate",
    )(gathered)
    return out.reshape(8, 2, 512, 512)


def per_device(voltages, pfb_taps, feed_flags):
    coarse, fine = phase_tables()
    flags = jnp.broadcast_to(feed_flags.astype(jnp.float32).reshape(2, OCT, 1), (2, OCT, LANES))
    return visibilities(gather_spectra(voltages, pfb_taps, flags, jnp.asarray(coarse), jnp.asarray(fine)))


def solution(mesh):
    return jax.shard_map(
        per_device,
        mesh=mesh,
        in_specs=(P("feed", "tm"), P(), P("feed")),
        out_specs=P(("feed", "tm"), None, None, None),
        check_vma=False,
    )
```

time: 288 us -> 92.8 us (0.32)
  the two profiles are of different devices: /device:TPU:7 before, /device:TPU:1 now
where the time goes in v1:
time: 92.8 us; the launch traced here: 92.6 us
  Pallas kernels  89 us (96%)
  local copies, waits for them, and re-layouts  3.01 us (3%)
    pallas_call x1, Pallas kernels, gather_spectra(): pl.pallas_call(channelise, out_shape=jax.ShapeDtypeStruct((2, 2, TIMES, F...  78.8 us
    pallas_call x1, Pallas kernels, visibilities(): pl.pallas_call(correlate, out_shape=jax.ShapeDtypeStruct((2, 2, 2, 2, 512...  10.1 us
    unnamed x6, local copies, waits for them, and re-layouts  2.85 us

profile of v1, /device:TPU:1, one launch (start us, length us, event | category | flops | bytes accessed | tf_op | source)
XLA Modules:
  0.0 92.6 jit_solution(16963619704956755819)
XLA Ops:
  0.0 0.7 convert_element_type.3
  0.7 0.1 broadcast_in_dim.7
  0.7 0.1 broadcast_in_dim.8.flag_ref
  0.8 0.0 copy-start
  0.8 1.0 %copy-done = f32[2,64,1024]{2,1,0:T(8,128)S(1)} copy-done((f32[2,64,1024]{2,1,0:T(8,128)S(1)}, f32[2,64,1024]{2,1,0:T(8,128)}, u32[]{:S(2)}) %copy-start) | copy-done | bytes 524312
  1.9 0.0 copy-start.1
  1.9 0.9 copy-done.1
  2.8 0.0 copy-start.2
  2.8 0.9 copy-done.2
  3.7 78.8 %channelise.1.block_ref = bf16[2,2,4,32,2,16,128]{6,5,4,3,2,1,0:T(8,128)(2,1)S(1)} custom-call(s32[16,131072]{1,0:T(8,128)} %volt_hbm.1, f32[16,2048]{1,0:T(8,128)S(1)} %copy-done.1, f32[2,8,128]{2,1,0:T(8,128)S(1)} %broadcast_in_dim.8.flag_ref, f32[2,64,1024]{2,1,0:T(8,128)S(1)} %copy-done, f32[2,2,8,1024]{3,2,1,0:T(8,128)S(1)} %copy-done.2), custom_call_target="tpu_custom_call" | custom-call | tf_op jit(solution)/shard_map/channelise/pallas_call | solution.py:280
  82.5 10.1 %correlate.1 = f32[2,2,2,2,512,512]{5,4,3,2,1,0:T(8,128)} custom-call(bf16[2,2,4,32,2,16,128]{6,5,4,3,2,1,0:T(8,128)(2,1)S(1)} %channelise.1.block_ref), custom_call_target="tpu_custom_call" | custom-call | tf_op jit(solution)/shard_map/correlate/pallas_call | solution.py:329
Async XLA Ops:
  0.8 1.0 %copy-start = (f32[2,64,1024]{2,1,0:T(8,128)S(1)}, f32[2,64,1024]{2,1,0:T(8,128)}, u32[]{:S(2)}) copy-start(f32[2,64,1024]{2,1,0:T(8,128)} %constant.4.clone.coarse_ref) | copy-start | bytes 1572868
  1.9 0.9 copy-start.1
  2.8 0.9 copy-start.2

commit v2 on v1

--- a/solution.py
+++ b/solution.py
@@ -81,24 +81,25 @@
 
 
 def channelise(
-    volt_hbm, taps_ref, flag_ref, coarse_ref, fine_ref, out_ref,
-    volt, edge, halo, table_hi, table_lo, folded, spectra, packed,
-    in_sem, halo_send, halo_recv, send_sem, recv_sem, own_sem,
+    volt_hbm, taps_hbm, flag_ref, coarse_hbm, fine_hbm, out_ref,
+    volt, taps_ref, coarse_ref, fine_ref, edge, halo, table_hi, table_lo, folded, spectra, packed,
+    in_sem, const_sem, halo_send, halo_recv, send_sem, recv_sem, own_sem,
 ):
     feed, time = lax.axis_index("feed"), lax.axis_index("tm")
     me = feed * TIMES + time
 
     tail = (SPEC - 16) * FRAME
-    loads = []
+    edges, bodies = [], []
     for o in range(2):
-        loads.append(pltpu.make_async_copy(
-            volt_hbm.at[pl.ds(o * OCT, OCT), pl.ds(tail, 16 * FRAME)],
-            volt.at[o, :, pl.ds(tail, 16 * FRAME)], in_sem.at[o, 0]))
-    for o in range(2):
-        loads.append(pltpu.make_async_copy(
-            volt_hbm.at[pl.ds(o * OCT, OCT), pl.ds(0, tail)],
-            volt.at[o, :, pl.ds(0, tail)], in_sem.at[o, 1]))
-    for load in loads:
+        inputs = pl.ds(o * OCT, OCT)
+        edges.append(pltpu.make_async_copy(
+            volt_hbm.at[inputs, pl.ds(tail, 16 * FRAME)], volt.at[o, :, pl.ds(tail, 16 * FRAME)], in_sem.at[o, 0]))
+        bodies.append(pltpu.make_async_copy(
+            volt_hbm.at[inputs, pl.ds(0, tail)], volt.at[o, :, pl.ds(0, tail)], in_sem.at[o, 1]))
+    fine_load = pltpu.make_async_copy(fine_hbm, fine_ref, const_sem.at[0])
+    coarse_load = pltpu.make_async_copy(coarse_hbm, coarse_ref, const_sem.at[1])
+    taps_load = pltpu.make_async_copy(taps_hbm, taps_ref, const_sem.at[2])
+    for load in (*edges, fine_load, coarse_load, taps_load, *bodies):
         load.start()
 
     barrier = pltpu.get_barrier_semaphore()
@@ -130,22 +131,27 @@
 
         lax.fori_loop(0, 32, rows, 0)
 
+    for o in range(2):
+        edges[o].wait()
+
+    @pl.when(time < TIMES - 1)
+    def _():
+        def pack_edge(nb, carry):
+            lanes = pl.ds(pl.multiple_of(nb * LANES, LANES), LANES)
+            for o in range(2):
+                for pair in range(8):
+                    two = []
+                    for side in range(2):
+                        at = pl.multiple_of(tail + (pair * 2 + side) * FRAME + nb * LANES, LANES)
+                        two.append(volt[o, :, pl.ds(at, LANES)].astype(jnp.float32))
+                    edge[o, pair, :, lanes] = jnp.concatenate(two, axis=0).astype(jnp.bfloat16)
+            return carry
+
+        lax.fori_loop(0, FRAME // LANES, pack_edge, 0)
+
+    fine_load.wait()
+    coarse_load.wait()
     make_table(0)
-
-    for o in range(2):
-        loads[o].wait()
-
-        def pack_edge(nb, carry, o=o):
-            for pair in range(8):
-                two = []
-                for side in range(2):
-                    at = pl.multiple_of(tail + (pair * 2 + side) * FRAME + nb * LANES, LANES)
-                    two.append(volt[o, :, pl.ds(at, LANES)].astype(jnp.float32))
-                lanes = pl.ds(pl.multiple_of(nb * LANES, LANES), LANES)
-                edge[o, pair, :, lanes] = jnp.concatenate(two, axis=0).astype(jnp.bfloat16)
-            return carry
-
-        lax.fori_loop(0, FRAME // LANES, pack_edge, 0)
 
     pl.semaphore_wait(barrier, DEVICES - 1)
 
@@ -163,45 +169,42 @@
     def _():
         halo[...] = jnp.zeros_like(halo)
 
-    def filter_block(o, mb, nb, first):
-        flag = flag_ref[o]
-        sides = []
-        for side in range(2):
-            lane0 = nb * LANES + side * HALF
-            lanes = pl.ds(pl.multiple_of(lane0, LANES), LANES)
-            taps = [jnp.broadcast_to(taps_ref[pl.ds(p, 1), lanes], (OCT, LANES)) for p in range(TAPS)]
-            sums = [None] * 16
-            early = None
-            for j in range(-15, 16):
-                if first and j < 0:
-                    pair, odd = (16 + j) // 2, (16 + j) % 2
-                    if odd == 0 or early is None:
-                        early = halo[o, pair, :, lanes].astype(jnp.float32)
-                    x = early[odd * OCT:(odd + 1) * OCT]
-                else:
-                    at = pl.multiple_of((mb * 16 + j) * FRAME + lane0, LANES)
-                    x = volt[o, :, pl.ds(at, LANES)].astype(jnp.float32)
-                for m in range(max(0, j), min(15, j + 15) + 1):
-                    term = taps[m - j] * x
-                    sums[m] = term if sums[m] is None else sums[m] + term
-            value = jnp.stack([s * flag for s in sums])
-            value = jnp.swapaxes(value, 0, 1)
-            sides.append(value.astype(jnp.bfloat16).astype(jnp.float32))
-        rows = pl.ds(pl.multiple_of(mb * 16, 16), 16)
-        lanes = pl.ds(pl.multiple_of(nb * LANES, LANES), LANES)
-        folded[o, 0, :, rows, lanes] = (sides[0] + sides[1]).astype(jnp.bfloat16)
-        folded[o, 1, :, rows, lanes] = (sides[0] - sides[1]).astype(jnp.bfloat16)
-
-    for o in range(2):
-        loads[2 + o].wait()
-
-    def later_blocks(step, carry):
-        o = step // (8 * (BLOCKS - 1))
-        rest = step % (8 * (BLOCKS - 1))
-        filter_block(o, 1 + rest // 8, rest % 8, False)
-        return carry
-
-    lax.fori_loop(0, 2 * 8 * (BLOCKS - 1), later_blocks, 0)
+    taps_load.wait()
+    sublane = lax.broadcasted_iota(jnp.int32, (OCT, LANES), 0)
+
+    def flags_of(o):
+        flag = jnp.zeros((OCT, LANES), jnp.float32)
+        for i in range(OCT):
+            flag = jnp.where(sublane == i, flag_ref[o * OCT + i].astype(jnp.float32), flag)
+        return flag
+
+    def filter_blocks(o, nb, flag, blocks):
+        for mb in blocks:
+            sides = []
+            for side in range(2):
+                lane0 = nb * LANES + side * HALF
+                lanes = pl.ds(pl.multiple_of(lane0, LANES), LANES)
+                taps = [jnp.broadcast_to(taps_ref[pl.ds(p, 1), lanes], (OCT, LANES)) for p in range(TAPS)]
+                sums = [None] * 16
+                early = None
+                for j in range(-15, 16):
+                    if mb == 0 and j < 0:
+                        pair, odd = (16 + j) // 2, (16 + j) % 2
+                        if odd == 0 or early is None:
+                            early = halo[o, pair, :, lanes].astype(jnp.float32)
+                        x = early[odd * OCT:(odd + 1) * OCT]
+                    else:
+                        at = pl.multiple_of((mb * 16 + j) * FRAME + lane0, LANES)
+                        x = volt[o, :, pl.ds(at, LANES)].astype(jnp.float32)
+                    for m in range(max(0, j), min(15, j + 15) + 1):
+                        term = taps[m - j] * x
+                        sums[m] = term if sums[m] is None else sums[m] + term
+                value = jnp.swapaxes(jnp.stack([s * flag for s in sums]), 0, 1)
+                sides.append(value.astype(jnp.bfloat16).astype(jnp.float32))
+            rows = slice(mb * 16, (mb + 1) * 16)
+            lanes = pl.ds(pl.multiple_of(nb * LANES, LANES), LANES)
+            folded[o, 0, :, rows, lanes] = (sides[0] + sides[1]).astype(jnp.bfloat16)
+            folded[o, 1, :, rows, lanes] = (sides[0] - sides[1]).astype(jnp.bfloat16)
 
     lane = lax.broadcasted_iota(jnp.int32, (8, LANES), 1)
     left_half = lane < SPEC
@@ -217,13 +220,23 @@
             packed.at[me, o, q], out_ref.at[q, pl.ds(0, 2), time, feed, o], own_sem)
 
     def octet(o, carry):
+        flag = flags_of(o)
+
+        def later_blocks(nb, c):
+            filter_blocks(o, nb, flag, range(1, BLOCKS))
+            return c
+
+        def first_block(nb, c):
+            filter_blocks(o, nb, flag, range(1))
+            return c
+
+        pltpu.make_async_copy(
+            volt_hbm.at[pl.ds(0, OCT), pl.ds(0, tail)], volt.at[o, :, pl.ds(0, tail)], in_sem.at[o, 1]).wait()
+        lax.fori_loop(0, 8, later_blocks, 0)
+
         @pl.when(time > 0)
         def _():
             halo_copy(o).wait_recv()
-
-        def first_block(nb, c):
-            filter_block(o, 0, nb, True)
-            return c
 
         lax.fori_loop(0, 8, first_block, 0)
 
@@ -251,7 +264,7 @@
                 packed[pl.ds(g * 2, 2), o, q] = tile.reshape(2, 2, 16, LANES).astype(jnp.bfloat16)
                 return c
 
-            lax.fori_loop(0, DEVICES // 2, turn, 0)
+            lax.fori_loop(0, DEVICES // 2, turn, 0, unroll=4)
             for offset in ORDER:
                 exchange(o, q, *peer(offset, feed, time)).start()
             own_copy(o, q).start()
@@ -276,14 +289,17 @@
 
 
 def gather_spectra(voltages, pfb_taps, flags, coarse, fine):
-    vmem = pl.BlockSpec(memory_space=pltpu.VMEM)
+    hbm = pl.BlockSpec(memory_space=pltpu.HBM)
     return pl.pallas_call(
         channelise,
         out_shape=jax.ShapeDtypeStruct((2, 2, TIMES, FEEDS, 2, 16, LANES), jnp.bfloat16),
-        in_specs=[pl.BlockSpec(memory_space=pl.ANY), vmem, vmem, vmem, vmem],
+        in_specs=[hbm, hbm, pl.BlockSpec(memory_space=pltpu.SMEM), hbm, hbm],
         out_specs=pl.BlockSpec(memory_space=pl.ANY),
         scratch_shapes=[
             pltpu.VMEM((2, OCT, SPEC * FRAME), jnp.int32),
+            pltpu.VMEM((TAPS, FRAME), jnp.float32),
+            pltpu.VMEM((2, 64, HALF), jnp.float32),
+            pltpu.VMEM((2, 2, 8, HALF), jnp.float32),
             pltpu.VMEM((2, 8, 16, FRAME), jnp.bfloat16),
             pltpu.VMEM((2, 8, 16, FRAME), jnp.bfloat16),
             pltpu.VMEM((2, 2, 512, HALF), jnp.bfloat16),
@@ -292,6 +308,7 @@
             pltpu.VMEM((2, 512, OCT * SPEC), jnp.float32),
             pltpu.VMEM((DEVICES, 2, 2, 2, 16, LANES), jnp.bfloat16),
             pltpu.SemaphoreType.DMA((2, 2)),
+            pltpu.SemaphoreType.DMA((3,)),
             pltpu.SemaphoreType.DMA((2,)),
             pltpu.SemaphoreType.DMA((2,)),
             pltpu.SemaphoreType.DMA,
@@ -304,36 +321,52 @@
     )(voltages, pfb_taps, flags, coarse, fine)
 
 
-def correlate(block_ref, out_ref, left, right):
-    which = pl.program_id(2)
-    lane = lax.broadcasted_iota(jnp.int32, (8, LANES), 1)
-
-    for other in range(2):
-        @pl.when(which == other)
-        def _():
+def correlate(spec, out_hbm, left, right, result, out_sem):
+    lane = lax.broadcasted_iota(jnp.int32, (1, LANES), 1)
+    sign = jnp.where(lane < SPEC, 1.0, -1.0)
+    dims = (((1,), (1,)), ((), ()))
+
+    def put(step, j, c):
+        q, p = step // 2, step % 2
+        slot = step * 4 + j * 2 + c
+        return pltpu.make_async_copy(result.at[slot], out_hbm.at[p, j, q, c], out_sem.at[slot])
+
+    def channels(step, carry):
+        q, p = step // 2, step % 2
+        for j in range(2):
             for t in range(TIMES):
-                tile = block_ref[0, 0, t].astype(jnp.float32)
-                tile = tile[:, :, other * OCT:(other + 1) * OCT, :].reshape(512, LANES)
+                tile = spec[q, p, t].astype(jnp.float32)
+                tile = tile[:, :, j * OCT:(j + 1) * OCT, :].reshape(512, LANES)
                 cols = slice(t * LANES, (t + 1) * LANES)
-                right[:, cols] = tile.astype(jnp.bfloat16)
-                sign = jnp.where(lane[:1] < SPEC, 1.0, -1.0)
-                left[:, cols] = (pltpu.roll(tile, SPEC, 1) * sign).astype(jnp.bfloat16)
-
-    dims = (((1,), (1,)), ((), ()))
-    value = right[...]
-    out_ref[0, 0, 0, 0] = lax.dot_general(value, value, dims, preferred_element_type=jnp.float32)
-    out_ref[0, 0, 0, 1] = lax.dot_general(left[...], value, dims, preferred_element_type=jnp.float32)
+                right[j, :, cols] = tile.astype(jnp.bfloat16)
+                left[j, :, cols] = (pltpu.roll(tile, SPEC, 1) * sign).astype(jnp.bfloat16)
+            value = right[j]
+            result[step * 4 + j * 2] = lax.dot_general(value, value, dims, preferred_element_type=jnp.float32)
+            put(step, j, 0).start()
+            result[step * 4 + j * 2 + 1] = lax.dot_general(left[j], value, dims, preferred_element_type=jnp.float32)
+            put(step, j, 1).start()
+        return carry
+
+    lax.fori_loop(0, 4, channels, 0)
+    for step in range(4):
+        for j in range(2):
+            for c in range(2):
+                put(step, j, c).wait()
 
 
 def visibilities(gathered):
     out = pl.pallas_call(
         correlate,
         out_shape=jax.ShapeDtypeStruct((2, 2, 2, 2, 512, 512), jnp.float32),
-        grid=(2, 2, 2),
-        in_specs=[pl.BlockSpec((1, 1, TIMES, FEEDS, 2, 16, LANES), lambda q, p, j: (q, p, 0, 0, 0, 0, 0))],
-        out_specs=pl.BlockSpec((1, 1, 1, 2, 512, 512), lambda q, p, j: (p, j, q, 0, 0, 0)),
-        scratch_shapes=[pltpu.VMEM((512, 512), jnp.bfloat16), pltpu.VMEM((512, 512), jnp.bfloat16)],
-        compiler_params=pltpu.CompilerParams(vmem_limit_bytes=32 << 20),
+        in_specs=[pl.BlockSpec(memory_space=pltpu.VMEM)],
+        out_specs=pl.BlockSpec(memory_space=pltpu.HBM),
+        scratch_shapes=[
+            pltpu.VMEM((2, 512, 512), jnp.bfloat16),
+            pltpu.VMEM((2, 512, 512), jnp.bfloat16),
+            pltpu.VMEM((16, 512, 512), jnp.float32),
+            pltpu.SemaphoreType.DMA((16,)),
+        ],
+        compiler_params=pltpu.CompilerParams(vmem_limit_bytes=48 << 20),
         name="correlate",
     )(gathered)
     return out.reshape(8, 2, 512, 512)
@@ -341,8 +374,11 @@
 
 def per_device(voltages, pfb_taps, feed_flags):
     coarse, fine = phase_tables()
-    flags = jnp.broadcast_to(feed_flags.astype(jnp.float32).reshape(2, OCT, 1), (2, OCT, LANES))
-    return visibilities(gather_spectra(voltages, pfb_taps, flags, jnp.asarray(coarse), jnp.asarray(fine)))
+    pinned = [
+        pltpu.with_memory_space_constraint(x, pltpu.HBM)
+        for x in (voltages, pfb_taps, feed_flags, jnp.asarray(coarse), jnp.asarray(fine))
+    ]
+    return visibilities(gather_spectra(*pinned))
 
 
 def solution(mesh):

time: 92.8 us -> 78 us (0.84)
  Pallas kernels: 89 us -> 77.9 us
  local copies, waits for them, and re-layouts: 3.01 us -> 0 us
    pallas_call x1, Pallas kernels: 78.8 us -> 71.3 us  [gather_spectra(): pl.pallas_call(channelise, out_shape=jax.ShapeDtypeStruct((2, 2, TIMES, F...]
    pallas_call x1, Pallas kernels: 10.1 us -> 6.62 us  [visibilities(): pl.pallas_call(correlate, out_shape=jax.ShapeDtypeStruct((2, 2, 2, 2, 512...]
    unnamed x6 -> x0, local copies, waits for them, and re-layouts: 2.85 us -> none
where the time goes in v2:
time: 78 us; the launch traced here: 77.9 us
  Pallas kernels  77.9 us (100%)
    pallas_call x1, Pallas kernels, gather_spectra(): pl.pallas_call(channelise, out_shape=jax.ShapeDtypeStruct((2, 2, TIMES, F...  71.3 us
    pallas_call x1, Pallas kernels, visibilities(): pl.pallas_call(correlate, out_shape=jax.ShapeDtypeStruct((2, 2, 2, 2, 512...  6.62 us

profile of v2, /device:TPU:1, one launch (start us, length us, event | category | flops | bytes accessed | tf_op | source)
XLA Modules:
  0.0 77.9 jit_solution(11194620586875255212)
XLA Ops:
  0.0 71.3 %channelise.1.spec = bf16[2,2,4,32,2,16,128]{6,5,4,3,2,1,0:T(8,128)(2,1)S(1)} custom-call(s32[16,131072]{1,0:T(8,128)} %volt_hbm.1, f32[16,2048]{1,0:T(8,128)} %taps_hbm.1, s32[16]{0:T(128)} %flag_ref.1, f32[2,64,1024]{2,1,0:T(8,128)} %constant.4.clone.coarse_hbm, f32[2,2,8,1024]{3,2,1,0:T(8,128)} %constant.5.clone.fine_hbm), custom_call_target="tpu_custom_call" | custom-call | tf_op jit(solution)/shard_map/channelise/pallas_call | solution.py:293
  71.3 6.6 %correlate.1 = f32[2,2,2,2,512,512]{5,4,3,2,1,0:T(8,128)} custom-call(bf16[2,2,4,32,2,16,128]{6,5,4,3,2,1,0:T(8,128)(2,1)S(1)} %channelise.1.spec), custom_call_target="tpu_custom_call" | custom-call | tf_op jit(solution)/shard_map/correlate/pallas_call | solution.py:358

commit v3 on v2

--- a/solution.py
+++ b/solution.py
@@ -21,58 +21,25 @@
 BLOCKS = SPEC // 16
 
 
-def link_loads(offset):
-    loads = [0] * 6
-    for axis, step in enumerate(offset[1:]):
-        if step in (1, 2):
-            loads[2 * axis] += 1
-        if step in (2, 3):
-            loads[2 * axis + 1] += 1
-    return loads
-
-
-def send_order():
-    left = [
-        (c, y, x, z)
-        for z in range(4)
-        for x in range(4)
-        for y in range(4)
-        for c in range(2)
-        if (c, y, x, z) != (0, 0, 0, 0)
-    ]
-    mixed = [left[(37 * i + 11) % len(left)] for i in range(len(left))]
-    order, total = [], [0] * 6
-    while mixed:
-        def spread(offset):
-            sums = [a + b for a, b in zip(total, link_loads(offset))]
-            mean = sum(sums) / 6
-            return sum((s - mean) ** 2 for s in sums)
-
-        best = min(mixed, key=spread)
-        mixed.remove(best)
-        order.append(best)
-        total = [a + b for a, b in zip(total, link_loads(best))]
-    return order
-
-
-ORDER = send_order()
-
-
-def peer(offset, feed, time):
-    dc, dy, dx, dz = offset
-    y = feed // 16 * 2 + time // 2
-    x = lax.rem(feed // 4 % 4 + dx, 4)
-    z = lax.rem(feed % 4 + dz, 4)
-    y = lax.rem(y + dy, 4)
-    c = lax.rem(time % 2 + dc, 2)
-    return y // 2 * 16 + x * 4 + z, y % 2 * 2 + c
+def peers(section, feed, time):
+    core, y, x, z = time % 2, feed // 16 * 2 + time // 2, feed // 4 % 4, feed % 4
+    cores = [lax.rem(core + i, 2) for i in range(2)]
+    ys = [lax.rem(y + i, 4) for i in range(4)]
+    ys = [(lax.div(v, 2) * 16, lax.rem(v, 2) * 2) for v in ys]
+    xs = [lax.rem(x + i, 4) * 4 for i in range(4)]
+    zs = [lax.rem(z + i + 3 * section, 4) for i in range(4)]
+    found = []
+    for i in range(32):
+        offset = i * 47 % DEVICES
+        y_feed, y_time = ys[offset // 2 % 4]
+        found.append((y_feed + xs[offset // 8 % 4] + zs[offset // 32], y_time + cores[offset % 2]))
+    return found
 
 
 def phase_tables():
     n = np.arange(HALF)
-    coarse = np.exp(-2j * np.pi * ((16 * np.arange(64)[:, None] * n) % FRAME) / FRAME)
-    rows = 8 * np.arange(2)[:, None] + 2 * np.arange(4)
-    rows = rows.reshape(8)[None, :, None] + np.arange(2)[:, None, None]
+    coarse = np.exp(-2j * np.pi * ((8 * np.arange(DEVICES)[:, None] * n) % FRAME) / FRAME)
+    rows = np.tile(2 * np.arange(4), 2)[None, :, None] + np.arange(2)[:, None, None]
     scale = 1.0 / (128 * 16 * math.sqrt(FRAME))
     fine = scale * np.exp(-2j * np.pi * (rows * n % FRAME) / FRAME)
     coarse = np.stack([coarse.real, coarse.imag]).astype(np.float32)
@@ -82,11 +49,10 @@
 
 def channelise(
     volt_hbm, taps_hbm, flag_ref, coarse_hbm, fine_hbm, out_ref,
-    volt, taps_ref, coarse_ref, fine_ref, edge, halo, table_hi, table_lo, folded, spectra, packed,
+    volt, taps_ref, coarse_ref, fine_ref, edge, halo, table, folded, spectra, packed,
     in_sem, const_sem, halo_send, halo_recv, send_sem, recv_sem, own_sem,
 ):
     feed, time = lax.axis_index("feed"), lax.axis_index("tm")
-    me = feed * TIMES + time
 
     tail = (SPEC - 16) * FRAME
     edges, bodies = [], []
@@ -104,66 +70,79 @@
 
     barrier = pltpu.get_barrier_semaphore()
 
-    def greet(step, carry):
-        other = lax.rem(me + step, DEVICES)
-        pl.semaphore_signal(barrier, inc=1, device_id=(other // TIMES, other % TIMES), device_id_type=MESH)
+    def greet(w, carry):
+        others = peers(w, feed, time)
+
+        @pl.when(w > 0)
+        def _():
+            pl.semaphore_signal(barrier, inc=1, device_id=others[0], device_id_type=MESH)
+
+        for other in others[1:]:
+            pl.semaphore_signal(barrier, inc=1, device_id=other, device_id_type=MESH)
         return carry
 
-    lax.fori_loop(1, DEVICES, greet, 0)
+    lax.fori_loop(0, 4, greet, 0)
+
+    upper = lax.broadcasted_iota(jnp.int32, (8, HALF), 0) < 4
 
     def make_table(q):
         fine_re, fine_im = fine_ref[q, 0], fine_ref[q, 1]
 
-        def rows(pair, carry):
-            parts = []
-            for side in range(2):
-                a_re = coarse_ref[0, pl.ds(pair * 2 + side, 1), :]
-                a_im = coarse_ref[1, pl.ds(pair * 2 + side, 1), :]
-                parts.append((a_re * fine_re - a_im * fine_im, a_re * fine_im + a_im * fine_re))
-            for c in range(2):
-                value = jnp.concatenate([parts[0][c], parts[1][c]], axis=0)
-                high = value.astype(jnp.bfloat16)
-                low = (value - high.astype(jnp.float32)).astype(jnp.bfloat16)
-                at = pl.ds(pl.multiple_of(pair * 16, 16), 16)
-                table_hi[q, c, at, :] = high
-                table_lo[q, c, at, :] = low
+        def rows(w, carry):
+            owners = [f * TIMES + t for f, t in peers(w, feed, time)]
+            for group in range(8):
+                parts = []
+                for side in range(2):
+                    two = owners[group * 4 + side * 2:group * 4 + side * 2 + 2]
+                    phase = [[coarse_ref[c, pl.ds(d, 1), :] for c in range(2)] for d in two]
+                    a_re, a_im = [jnp.where(upper, phase[0][c], phase[1][c]) for c in range(2)]
+                    parts.append((a_re * fine_re - a_im * fine_im, a_re * fine_im + a_im * fine_re))
+                for c in range(2):
+                    value = jnp.concatenate([parts[0][c], parts[1][c]], axis=0)
+                    high = value.astype(jnp.bfloat16)
+                    low = (value - high.astype(jnp.float32)).astype(jnp.bfloat16)
+                    table[q, w, 0, c, group * 16:(group + 1) * 16, :] = high
+                    table[q, w, 1, c, group * 16:(group + 1) * 16, :] = low
             return carry
 
-        lax.fori_loop(0, 32, rows, 0)
-
-    for o in range(2):
-        edges[o].wait()
-
-    @pl.when(time < TIMES - 1)
-    def _():
-        def pack_edge(nb, carry):
-            lanes = pl.ds(pl.multiple_of(nb * LANES, LANES), LANES)
-            for o in range(2):
-                for pair in range(8):
-                    two = []
-                    for side in range(2):
-                        at = pl.multiple_of(tail + (pair * 2 + side) * FRAME + nb * LANES, LANES)
-                        two.append(volt[o, :, pl.ds(at, LANES)].astype(jnp.float32))
-                    edge[o, pair, :, lanes] = jnp.concatenate(two, axis=0).astype(jnp.bfloat16)
-            return carry
-
-        lax.fori_loop(0, FRAME // LANES, pack_edge, 0)
-
-    fine_load.wait()
-    coarse_load.wait()
-    make_table(0)
-
-    pl.semaphore_wait(barrier, DEVICES - 1)
+        lax.fori_loop(0, 4, rows, 0)
 
     def halo_copy(o):
         return pltpu.make_async_remote_copy(
             src_ref=edge.at[o], dst_ref=halo.at[o], send_sem=halo_send.at[o], recv_sem=halo_recv.at[o],
             device_id=(feed, lax.rem(time + 1, TIMES)), device_id_type=MESH)
 
+    def pack_edge(o):
+        def block(nb, carry):
+            lanes = pl.ds(pl.multiple_of(nb * LANES, LANES), LANES)
+            for pair in range(8):
+                two = []
+                for side in range(2):
+                    at = pl.multiple_of(tail + (pair * 2 + side) * FRAME + nb * LANES, LANES)
+                    two.append(volt[o, :, pl.ds(at, LANES)].astype(jnp.float32))
+                edge[o, pair, :, lanes] = jnp.concatenate(two, axis=0).astype(jnp.bfloat16)
+            return carry
+
+        lax.fori_loop(0, FRAME // LANES, block, 0)
+
+    edges[0].wait()
+
     @pl.when(time < TIMES - 1)
     def _():
-        for o in range(2):
-            halo_copy(o).start()
+        pack_edge(0)
+
+    pl.semaphore_wait(barrier, DEVICES - 1)
+    edges[1].wait()
+
+    @pl.when(time < TIMES - 1)
+    def _():
+        halo_copy(0).start()
+        pack_edge(1)
+        halo_copy(1).start()
+
+    fine_load.wait()
+    coarse_load.wait()
+    make_table(0)
 
     @pl.when(time == 0)
     def _():
@@ -209,15 +188,13 @@
     lane = lax.broadcasted_iota(jnp.int32, (8, LANES), 1)
     left_half = lane < SPEC
 
-    def exchange(o, q, other_feed, other_time):
+    def exchange(o, q, step, other):
         return pltpu.make_async_remote_copy(
-            src_ref=packed.at[other_feed * TIMES + other_time, o, q],
-            dst_ref=out_ref.at[q, pl.ds(0, 2), time, feed, o],
-            send_sem=send_sem, recv_sem=recv_sem, device_id=(other_feed, other_time), device_id_type=MESH)
+            src_ref=packed.at[step, o, q], dst_ref=out_ref.at[q, pl.ds(0, 2), time, feed, o],
+            send_sem=send_sem, recv_sem=recv_sem, device_id=other, device_id_type=MESH)
 
     def own_copy(o, q):
-        return pltpu.make_async_copy(
-            packed.at[me, o, q], out_ref.at[q, pl.ds(0, 2), time, feed, o], own_sem)
+        return pltpu.make_async_copy(packed.at[0, o, q], out_ref.at[q, pl.ds(0, 2), time, feed, o], own_sem)
 
     def octet(o, carry):
         flag = flags_of(o)
@@ -245,29 +222,42 @@
             def _():
                 make_table(1)
 
-            right = folded[o, q].reshape(OCT * SPEC, HALF)
-            dims = (((1,), (1,)), ((), ()))
-            for c in range(2):
-                spectra[c] = lax.dot_general(
-                    table_hi[q, c], right, dims, preferred_element_type=jnp.float32
-                ) + lax.dot_general(table_lo[q, c], right, dims, preferred_element_type=jnp.float32)
-
-            def turn(g, c):
-                rows = pl.ds(pl.multiple_of(g * 8, 8), 8)
-                tiles = []
-                for pair in range(OCT // 2):
-                    re = spectra[0, rows, pair * LANES:(pair + 1) * LANES]
-                    im = spectra[1, rows, pair * LANES:(pair + 1) * LANES]
-                    tiles.append(jnp.where(left_half, re, pltpu.roll(im, SPEC, 1)))
-                    tiles.append(jnp.where(left_half, pltpu.roll(re, SPEC, 1), im))
-                tile = jnp.swapaxes(jnp.stack(tiles), 0, 1)
-                packed[pl.ds(g * 2, 2), o, q] = tile.reshape(2, 2, 16, LANES).astype(jnp.bfloat16)
-                return c
-
-            lax.fori_loop(0, DEVICES // 2, turn, 0, unroll=4)
-            for offset in ORDER:
-                exchange(o, q, *peer(offset, feed, time)).start()
-            own_copy(o, q).start()
+            def section(w, carry):
+                right = folded[o, q].reshape(OCT * SPEC, HALF)
+                spectra[...] = lax.dot_general(
+                    table[q, w].reshape(512, HALF), right, (((1,), (1,)), ((), ())),
+                    preferred_element_type=jnp.float32).reshape(2, 2, 128, OCT * SPEC)
+
+                def turn(g, c):
+                    rows = pl.ds(pl.multiple_of(g * 8, 8), 8)
+                    tiles = []
+                    for pair in range(OCT // 2):
+                        lanes = slice(pair * LANES, (pair + 1) * LANES)
+                        re = spectra[0, 0, rows, lanes] + spectra[1, 0, rows, lanes]
+                        im = spectra[0, 1, rows, lanes] + spectra[1, 1, rows, lanes]
+                        tiles.append(jnp.where(left_half, re, pltpu.roll(im, SPEC, 1)))
+                        tiles.append(jnp.where(left_half, pltpu.roll(re, SPEC, 1), im))
+                    tile = jnp.swapaxes(jnp.stack(tiles), 0, 1)
+                    packed[pl.ds(w * 32 + g * 2, 2), o, q] = tile.reshape(2, 2, 16, LANES).astype(jnp.bfloat16)
+                    return c
+
+                lax.fori_loop(0, 16, turn, 0, unroll=True)
+
+                @pl.when(w == 0)
+                def _():
+                    own_copy(o, q).start()
+
+                others = peers(w, feed, time)
+
+                @pl.when(w > 0)
+                def _():
+                    exchange(o, q, w * 32, others[0]).start()
+
+                for i in range(1, 32):
+                    exchange(o, q, w * 32 + i, others[i]).start()
+                return carry
+
+            lax.fori_loop(0, 4, section, 0)
             return carry
 
         lax.fori_loop(0, 2, parity, 0)
@@ -298,14 +288,13 @@
         scratch_shapes=[
             pltpu.VMEM((2, OCT, SPEC * FRAME), jnp.int32),
             pltpu.VMEM((TAPS, FRAME), jnp.float32),
-            pltpu.VMEM((2, 64, HALF), jnp.float32),
+            pltpu.VMEM((2, DEVICES, HALF), jnp.float32),
             pltpu.VMEM((2, 2, 8, HALF), jnp.float32),
             pltpu.VMEM((2, 8, 16, FRAME), jnp.bfloat16),
             pltpu.VMEM((2, 8, 16, FRAME), jnp.bfloat16),
-            pltpu.VMEM((2, 2, 512, HALF), jnp.bfloat16),
-            pltpu.VMEM((2, 2, 512, HALF), jnp.bfloat16),
+            pltpu.VMEM((2, 4, 2, 2, 128, HALF), jnp.bfloat16),
             pltpu.VMEM((2, 2, OCT, SPEC, HALF), jnp.bfloat16),
-            pltpu.VMEM((2, 512, OCT * SPEC), jnp.float32),
+            pltpu.VMEM((2, 2, 128, OCT * SPEC), jnp.float32),
             pltpu.VMEM((DEVICES, 2, 2, 2, 16, LANES), jnp.bfloat16),
             pltpu.SemaphoreType.DMA((2, 2)),
             pltpu.SemaphoreType.DMA((3,)),

time: 78 us -> 77.7 us (level)
  no operation moved by 1% of the time
where the time goes in v3:
time: 77.7 us; the launch traced here: 77.6 us
  Pallas kernels  77.5 us (100%)
    pallas_call x1, Pallas kernels, gather_spectra(): pl.pallas_call(channelise, out_shape=jax.ShapeDtypeStruct((2, 2, TIMES, F...  70.9 us
    pallas_call x1, Pallas kernels, visibilities(): pl.pallas_call(correlate, out_shape=jax.ShapeDtypeStruct((2, 2, 2, 2, 512...  6.62 us

profile of v3, /device:TPU:1, one launch (start us, length us, event | category | flops | bytes accessed | tf_op | source)
XLA Modules:
  0.0 77.6 jit_solution(11949038585119308781)
XLA Ops:
  0.0 70.9 %channelise.1.spec = bf16[2,2,4,32,2,16,128]{6,5,4,3,2,1,0:T(8,128)(2,1)S(1)} custom-call(s32[16,131072]{1,0:T(8,128)} %volt_hbm.1, f32[16,2048]{1,0:T(8,128)} %taps_hbm.1, s32[16]{0:T(128)} %flag_ref.1, f32[2,128,1024]{2,1,0:T(8,128)} %constant.4.clone.coarse_hbm, f32[2,2,8,1024]{3,2,1,0:T(8,128)} %constant.5.clone.fine_hbm), custom_call_target="tpu_custom_call" | custom-call | tf_op jit(solution)/shard_map/channelise/pallas_call | solution.py:283
  70.9 6.6 %correlate.1 = f32[2,2,2,2,512,512]{5,4,3,2,1,0:T(8,128)} custom-call(bf16[2,2,4,32,2,16,128]{6,5,4,3,2,1,0:T(8,128)(2,1)S(1)} %channelise.1.spec), custom_call_target="tpu_custom_call" | custom-call | tf_op jit(solution)/shard_map/correlate/pallas_call | solution.py:347

commit v4 on v3

--- a/solution.py
+++ b/solution.py
@@ -112,6 +112,14 @@
             src_ref=edge.at[o], dst_ref=halo.at[o], send_sem=halo_send.at[o], recv_sem=halo_recv.at[o],
             device_id=(feed, lax.rem(time + 1, TIMES)), device_id_type=MESH)
 
+    across = lax.rem(feed + FEEDS // 2, FEEDS)
+    relay = pltpu.make_async_remote_copy(
+        src_ref=edge.at[1], dst_ref=edge.at[1], send_sem=halo_send.at[1], recv_sem=halo_recv.at[2],
+        device_id=(across, 3), device_id_type=MESH)
+    forward = pltpu.make_async_remote_copy(
+        src_ref=edge.at[1], dst_ref=halo.at[1], send_sem=halo_send.at[1], recv_sem=halo_recv.at[1],
+        device_id=(across, 2), device_id_type=MESH)
+
     def pack_edge(o):
         def block(nb, carry):
             lanes = pl.ds(pl.multiple_of(nb * LANES, LANES), LANES)
@@ -138,7 +146,14 @@
     def _():
         halo_copy(0).start()
         pack_edge(1)
+
+    @pl.when((time == 0) | (time == 2))
+    def _():
         halo_copy(1).start()
+
+    @pl.when(time == 1)
+    def _():
+        relay.start()
 
     fine_load.wait()
     coarse_load.wait()
@@ -211,6 +226,11 @@
             volt_hbm.at[pl.ds(0, OCT), pl.ds(0, tail)], volt.at[o, :, pl.ds(0, tail)], in_sem.at[o, 1]).wait()
         lax.fori_loop(0, 8, later_blocks, 0)
 
+        @pl.when((time == 3) & (o == 0))
+        def _():
+            relay.wait_recv()
+            forward.start()
+
         @pl.when(time > 0)
         def _():
             halo_copy(o).wait_recv()
@@ -267,8 +287,9 @@
 
     @pl.when(time < TIMES - 1)
     def _():
-        for o in range(2):
-            halo_copy(o).wait_send()
+        halo_copy(0).wait_send()
+
+    forward.wait_send()
 
     everything = pltpu.make_async_remote_copy(
         src_ref=packed.at[pl.ds(0, DEVICES - 1)], dst_ref=packed.at[pl.ds(0, DEVICES - 1)],
@@ -299,7 +320,7 @@
             pltpu.SemaphoreType.DMA((2, 2)),
             pltpu.SemaphoreType.DMA((3,)),
             pltpu.SemaphoreType.DMA((2,)),
-            pltpu.SemaphoreType.DMA((2,)),
+            pltpu.SemaphoreType.DMA((3,)),
             pltpu.SemaphoreType.DMA,
             pltpu.SemaphoreType.DMA,
             pltpu.SemaphoreType.DMA,

time: 77.7 us -> 79.9 us (1.028); the launches traced: 77.6 us -> 78.8 us
  Pallas kernels: 77.5 us -> 78.8 us
    pallas_call x1, Pallas kernels: 70.9 us -> 72.1 us  [gather_spectra(): pl.pallas_call(channelise, out_shape=jax.ShapeDtypeStruct((2, 2, TIMES, F...]
where the time goes in v4:
time: 79.9 us; the launch traced here: 78.8 us
  Pallas kernels  78.8 us (99%)
    pallas_call x1, Pallas kernels, gather_spectra(): pl.pallas_call(channelise, out_shape=jax.ShapeDtypeStruct((2, 2, TIMES, F...  72.1 us
    pallas_call x1, Pallas kernels, visibilities(): pl.pallas_call(correlate, out_shape=jax.ShapeDtypeStruct((2, 2, 2, 2, 512...  6.62 us

profile of v4, /device:TPU:1, one launch (start us, length us, event | category | flops | bytes accessed | tf_op | source)
XLA Modules:
  0.0 78.8 jit_solution(7094655443725054651)
XLA Ops:
  0.0 72.1 %channelise.1.spec = bf16[2,2,4,32,2,16,128]{6,5,4,3,2,1,0:T(8,128)(2,1)S(1)} custom-call(s32[16,131072]{1,0:T(8,128)} %volt_hbm.1, f32[16,2048]{1,0:T(8,128)} %taps_hbm.1, s32[16]{0:T(128)} %flag_ref.1, f32[2,128,1024]{2,1,0:T(8,128)} %constant.4.clone.coarse_hbm, f32[2,2,8,1024]{3,2,1,0:T(8,128)} %constant.5.clone.fine_hbm), custom_call_target="tpu_custom_call" | custom-call | tf_op jit(solution)/shard_map/channelise/pallas_call | solution.py:304
  72.1 6.6 %correlate.1 = f32[2,2,2,2,512,512]{5,4,3,2,1,0:T(8,128)} custom-call(bf16[2,2,4,32,2,16,128]{6,5,4,3,2,1,0:T(8,128)(2,1)S(1)} %channelise.1.spec), custom_call_target="tpu_custom_call" | custom-call | tf_op jit(solution)/shard_map/correlate/pallas_call | solution.py:368

commit v5 on v4

--- a/solution.py
+++ b/solution.py
@@ -19,6 +19,7 @@
 SPEC = 64
 OCT = 8
 BLOCKS = SPEC // 16
+DETOUR = 5
 
 
 def peers(section, feed, time):
@@ -113,12 +114,16 @@
             device_id=(feed, lax.rem(time + 1, TIMES)), device_id_type=MESH)
 
     across = lax.rem(feed + FEEDS // 2, FEEDS)
+    detour, straight = pl.ds(0, DETOUR), pl.ds(DETOUR, 8 - DETOUR)
     relay = pltpu.make_async_remote_copy(
-        src_ref=edge.at[1], dst_ref=edge.at[1], send_sem=halo_send.at[1], recv_sem=halo_recv.at[2],
-        device_id=(across, 3), device_id_type=MESH)
+        src_ref=edge.at[1, detour], dst_ref=edge.at[1, detour],
+        send_sem=halo_send.at[2], recv_sem=halo_recv.at[2], device_id=(across, 3), device_id_type=MESH)
     forward = pltpu.make_async_remote_copy(
-        src_ref=edge.at[1], dst_ref=halo.at[1], send_sem=halo_send.at[1], recv_sem=halo_recv.at[1],
-        device_id=(across, 2), device_id_type=MESH)
+        src_ref=edge.at[1, detour], dst_ref=halo.at[1, detour],
+        send_sem=halo_send.at[2], recv_sem=halo_recv.at[1], device_id=(across, 2), device_id_type=MESH)
+    rest = pltpu.make_async_remote_copy(
+        src_ref=edge.at[1, straight], dst_ref=halo.at[1, straight],
+        send_sem=halo_send.at[1], recv_sem=halo_recv.at[1], device_id=(feed, 2), device_id_type=MESH)
 
     def pack_edge(o):
         def block(nb, carry):
@@ -154,6 +159,7 @@
     @pl.when(time == 1)
     def _():
         relay.start()
+        rest.start()
 
     fine_load.wait()
     coarse_load.wait()
@@ -289,7 +295,18 @@
     def _():
         halo_copy(0).wait_send()
 
-    forward.wait_send()
+    @pl.when((time == 0) | (time == 2))
+    def _():
+        halo_copy(1).wait_send()
+
+    @pl.when(time == 1)
+    def _():
+        relay.wait_send()
+        rest.wait_send()
+
+    @pl.when(time == 3)
+    def _():
+        forward.wait_send()
 
     everything = pltpu.make_async_remote_copy(
         src_ref=packed.at[pl.ds(0, DEVICES - 1)], dst_ref=packed.at[pl.ds(0, DEVICES - 1)],
@@ -319,7 +336,7 @@
             pltpu.VMEM((DEVICES, 2, 2, 2, 16, LANES), jnp.bfloat16),
             pltpu.SemaphoreType.DMA((2, 2)),
             pltpu.SemaphoreType.DMA((3,)),
-            pltpu.SemaphoreType.DMA((2,)),
+            pltpu.SemaphoreType.DMA((3,)),
             pltpu.SemaphoreType.DMA((3,)),
             pltpu.SemaphoreType.DMA,
             pltpu.SemaphoreType.DMA,

time: 79.9 us -> 75.9 us (0.950); the launches traced: 78.8 us -> 75.8 us
  Pallas kernels: 78.8 us -> 75.8 us
    pallas_call x1, Pallas kernels: 72.1 us -> 69.2 us  [gather_spectra(): pl.pallas_call(channelise, out_shape=jax.ShapeDtypeStruct((2, 2, TIMES, F...]
where the time goes in v5:
time: 75.9 us; the launch traced here: 75.8 us
  Pallas kernels  75.8 us (100%)
    pallas_call x1, Pallas kernels, gather_spectra(): pl.pallas_call(channelise, out_shape=jax.ShapeDtypeStruct((2, 2, TIMES, F...  69.2 us
    pallas_call x1, Pallas kernels, visibilities(): pl.pallas_call(correlate, out_shape=jax.ShapeDtypeStruct((2, 2, 2, 2, 512...  6.62 us

profile of v5, /device:TPU:1, one launch (start us, length us, event | category | flops | bytes accessed | tf_op | source)
XLA Modules:
  0.0 75.8 jit_solution(357366394847409152)
XLA Ops:
  0.0 69.2 %channelise.1.spec = bf16[2,2,4,32,2,16,128]{6,5,4,3,2,1,0:T(8,128)(2,1)S(1)} custom-call(s32[16,131072]{1,0:T(8,128)} %volt_hbm.1, f32[16,2048]{1,0:T(8,128)} %taps_hbm.1, s32[16]{0:T(128)} %flag_ref.1, f32[2,128,1024]{2,1,0:T(8,128)} %constant.4.clone.coarse_hbm, f32[2,2,8,1024]{3,2,1,0:T(8,128)} %constant.5.clone.fine_hbm), custom_call_target="tpu_custom_call" | custom-call | tf_op jit(solution)/shard_map/channelise/pallas_call | solution.py:321
  69.2 6.6 %correlate.1 = f32[2,2,2,2,512,512]{5,4,3,2,1,0:T(8,128)} custom-call(bf16[2,2,4,32,2,16,128]{6,5,4,3,2,1,0:T(8,128)(2,1)S(1)} %channelise.1.spec), custom_call_target="tpu_custom_call" | custom-call | tf_op jit(solution)/shard_map/correlate/pallas_call | solution.py:385

commit v6 on v5

--- a/solution.py
+++ b/solution.py
@@ -46,6 +46,31 @@
     coarse = np.stack([coarse.real, coarse.imag]).astype(np.float32)
     fine = np.stack([fine.real, fine.imag], axis=1).astype(np.float32)
     return coarse, fine
+
+
+def fir(taps, x, first, last):
+    sums = {}
+    for m in range(first, last + 1):
+        total = taps[0] * x[m]
+        for p in range(1, len(taps)):
+            total = total + taps[p] * x[m - p]
+        sums[m] = total
+    return sums
+
+
+def fast_fir(taps, x):
+    h0, h1 = taps[0::2], taps[1::2]
+    x0 = {j // 2: v for j, v in x.items() if j % 2 == 0}
+    x1 = {j // 2: v for j, v in x.items() if j % 2 == 1}
+    both = {r: x0[r] + x1[r] for r in range(-7, 8)}
+    even = fir(h0, x0, 0, 7)
+    odd = fir(h1, x1, -1, 7)
+    mixed = fir([a + b for a, b in zip(h0, h1)], both, 0, 7)
+    sums = []
+    for r in range(8):
+        sums.append(even[r] + odd[r - 1])
+        sums.append(mixed[r] - (even[r] + odd[r]))
+    return sums
 
 
 def channelise(
@@ -185,20 +210,15 @@
                 lane0 = nb * LANES + side * HALF
                 lanes = pl.ds(pl.multiple_of(lane0, LANES), LANES)
                 taps = [jnp.broadcast_to(taps_ref[pl.ds(p, 1), lanes], (OCT, LANES)) for p in range(TAPS)]
-                sums = [None] * 16
-                early = None
+                x = {}
                 for j in range(-15, 16):
                     if mb == 0 and j < 0:
                         pair, odd = (16 + j) // 2, (16 + j) % 2
-                        if odd == 0 or early is None:
-                            early = halo[o, pair, :, lanes].astype(jnp.float32)
-                        x = early[odd * OCT:(odd + 1) * OCT]
+                        x[j] = halo[o, pair, :, lanes].astype(jnp.float32)[odd * OCT:(odd + 1) * OCT]
                     else:
                         at = pl.multiple_of((mb * 16 + j) * FRAME + lane0, LANES)
-                        x = volt[o, :, pl.ds(at, LANES)].astype(jnp.float32)
-                    for m in range(max(0, j), min(15, j + 15) + 1):
-                        term = taps[m - j] * x
-                        sums[m] = term if sums[m] is None else sums[m] + term
+                        x[j] = volt[o, :, pl.ds(at, LANES)].astype(jnp.float32)
+                sums = fast_fir(taps, x)
                 value = jnp.swapaxes(jnp.stack([s * flag for s in sums]), 0, 1)
                 sides.append(value.astype(jnp.bfloat16).astype(jnp.float32))
             rows = slice(mb * 16, (mb + 1) * 16)

time: 75.9 us -> 76 us (level)
  no operation moved by 1% of the time
where the time goes in v6:
time: 76 us; the launch traced here: 75.6 us
  Pallas kernels  75.6 us (99%)
    pallas_call x1, Pallas kernels, gather_spectra(): pl.pallas_call(channelise, out_shape=jax.ShapeDtypeStruct((2, 2, TIMES, F...  68.9 us
    pallas_call x1, Pallas kernels, visibilities(): pl.pallas_call(correlate, out_shape=jax.ShapeDtypeStruct((2, 2, 2, 2, 512...  6.61 us

profile of v6, /device:TPU:1, one launch (start us, length us, event | category | flops | bytes accessed | tf_op | source)
XLA Modules:
  0.0 75.6 jit_solution(6087705060228742097)
XLA Ops:
  0.0 68.9 %channelise.1.spec = bf16[2,2,4,32,2,16,128]{6,5,4,3,2,1,0:T(8,128)(2,1)S(1)} custom-call(s32[16,131072]{1,0:T(8,128)} %volt_hbm.1, f32[16,2048]{1,0:T(8,128)} %taps_hbm.1, s32[16]{0:T(128)} %flag_ref.1, f32[2,128,1024]{2,1,0:T(8,128)} %constant.4.clone.coarse_hbm, f32[2,2,8,1024]{3,2,1,0:T(8,128)} %constant.5.clone.fine_hbm), custom_call_target="tpu_custom_call" | custom-call | tf_op jit(solution)/shard_map/channelise/pallas_call | solution.py:341
  69.0 6.6 %correlate.1 = f32[2,2,2,2,512,512]{5,4,3,2,1,0:T(8,128)} custom-call(bf16[2,2,4,32,2,16,128]{6,5,4,3,2,1,0:T(8,128)(2,1)S(1)} %channelise.1.spec), custom_call_target="tpu_custom_call" | custom-call | tf_op jit(solution)/shard_map/correlate/pallas_call | solution.py:405

commit v7 on v6

--- a/solution.py
+++ b/solution.py
@@ -184,7 +184,6 @@
     @pl.when(time == 1)
     def _():
         relay.start()
-        rest.start()
 
     fine_load.wait()
     coarse_load.wait()
@@ -251,6 +250,10 @@
         pltpu.make_async_copy(
             volt_hbm.at[pl.ds(0, OCT), pl.ds(0, tail)], volt.at[o, :, pl.ds(0, tail)], in_sem.at[o, 1]).wait()
         lax.fori_loop(0, 8, later_blocks, 0)
+
+        @pl.when((time == 1) & (o == 0))
+        def _():
+            rest.start()
 
         @pl.when((time == 3) & (o == 0))
         def _():

time: 76 us -> 76 us (level)
  no operation moved by 1% of the time
where the time goes in v7:
time: 76 us; the launch traced here: 75.6 us
  Pallas kernels  75.6 us (99%)
    pallas_call x1, Pallas kernels, gather_spectra(): pl.pallas_call(channelise, out_shape=jax.ShapeDtypeStruct((2, 2, TIMES, F...  68.9 us
    pallas_call x1, Pallas kernels, visibilities(): pl.pallas_call(correlate, out_shape=jax.ShapeDtypeStruct((2, 2, 2, 2, 512...  6.62 us

profile of v7, /device:TPU:1, one launch (start us, length us, event | category | flops | bytes accessed | tf_op | source)
XLA Modules:
  0.0 75.6 jit_solution(7559820933600548647)
XLA Ops:
  0.0 68.9 %channelise.1.spec = bf16[2,2,4,32,2,16,128]{6,5,4,3,2,1,0:T(8,128)(2,1)S(1)} custom-call(s32[16,131072]{1,0:T(8,128)} %volt_hbm.1, f32[16,2048]{1,0:T(8,128)} %taps_hbm.1, s32[16]{0:T(128)} %flag_ref.1, f32[2,128,1024]{2,1,0:T(8,128)} %constant.4.clone.coarse_hbm, f32[2,2,8,1024]{3,2,1,0:T(8,128)} %constant.5.clone.fine_hbm), custom_call_target="tpu_custom_call" | custom-call | tf_op jit(solution)/shard_map/channelise/pallas_call | solution.py:344
  69.0 6.6 %correlate.1 = f32[2,2,2,2,512,512]{5,4,3,2,1,0:T(8,128)} custom-call(bf16[2,2,4,32,2,16,128]{6,5,4,3,2,1,0:T(8,128)(2,1)S(1)} %channelise.1.spec), custom_call_target="tpu_custom_call" | custom-call | tf_op jit(solution)/shard_map/correlate/pallas_call | solution.py:408

commit v8 on v7

--- a/solution.py
+++ b/solution.py
@@ -169,25 +169,25 @@
     def _():
         pack_edge(0)
 
-    pl.semaphore_wait(barrier, DEVICES - 1)
-    edges[1].wait()
-
-    @pl.when(time < TIMES - 1)
-    def _():
-        halo_copy(0).start()
-        pack_edge(1)
-
-    @pl.when((time == 0) | (time == 2))
-    def _():
-        halo_copy(1).start()
-
-    @pl.when(time == 1)
-    def _():
-        relay.start()
-
     fine_load.wait()
     coarse_load.wait()
     make_table(0)
+
+    pl.semaphore_wait(barrier, DEVICES - 1)
+    edges[1].wait()
+
+    @pl.when(time < TIMES - 1)
+    def _():
+        halo_copy(0).start()
+        pack_edge(1)
+
+    @pl.when((time == 0) | (time == 2))
+    def _():
+        halo_copy(1).start()
+
+    @pl.when(time == 1)
+    def _():
+        relay.start()
 
     @pl.when(time == 0)
     def _():

time: 76 us -> 76.1 us (level)
  no operation moved by 1% of the time
where the time goes in v8:
time: 76.1 us; the launch traced here: 75.5 us
  Pallas kernels  75.5 us (99%)
    pallas_call x1, Pallas kernels, gather_spectra(): pl.pallas_call(channelise, out_shape=jax.ShapeDtypeStruct((2, 2, TIMES, F...  68.8 us
    pallas_call x1, Pallas kernels, visibilities(): pl.pallas_call(correlate, out_shape=jax.ShapeDtypeStruct((2, 2, 2, 2, 512...  6.62 us

profile of v8, /device:TPU:1, one launch (start us, length us, event | category | flops | bytes accessed | tf_op | source)
XLA Modules:
  0.0 75.5 jit_solution(7050114958265522264)
XLA Ops:
  0.0 68.8 %channelise.1.spec = bf16[2,2,4,32,2,16,128]{6,5,4,3,2,1,0:T(8,128)(2,1)S(1)} custom-call(s32[16,131072]{1,0:T(8,128)} %volt_hbm.1, f32[16,2048]{1,0:T(8,128)} %taps_hbm.1, s32[16]{0:T(128)} %flag_ref.1, f32[2,128,1024]{2,1,0:T(8,128)} %constant.4.clone.coarse_hbm, f32[2,2,8,1024]{3,2,1,0:T(8,128)} %constant.5.clone.fine_hbm), custom_call_target="tpu_custom_call" | custom-call | tf_op jit(solution)/shard_map/channelise/pallas_call | solution.py:344
  68.9 6.6 %correlate.1 = f32[2,2,2,2,512,512]{5,4,3,2,1,0:T(8,128)} custom-call(bf16[2,2,4,32,2,16,128]{6,5,4,3,2,1,0:T(8,128)(2,1)S(1)} %channelise.1.spec), custom_call_target="tpu_custom_call" | custom-call | tf_op jit(solution)/shard_map/correlate/pallas_call | solution.py:408
